TPU v7x, 1024 devices: a whole 8x8x8 slice. The times are simulated.
1024 devices in a mesh: grp: 128 (over z, y, core), mem: 8 (over x).
Axes of the slice: x: 8, y: 8, z: 8, core: 2. Of those that a mesh axis runs over, the one named last changes fastest.
Arguments:
- wave: float32 [2, 512, 256, 256], P(None, 'grp', 'mem'), may hold values from -6 to 6
- beam_offsets: float32 [3, 128, 8, 1024], P(None, 'grp', 'mem'), may hold values from 0 to 1
- beam_waves: float32 [3, 128, 8, 1024], P(None, 'grp', 'mem'), may hold values from -3.140625 to 3.140625
- beam_amps: float32 [2, 128, 8, 1024], P(None, 'grp', 'mem'), may hold values from -6 to 6
- beam_widths: float32 [128, 8, 1024], P('grp', 'mem'), may hold values from 1.2 to 3
- beam_tile: int32 [128, 8, 1024], P('grp', 'mem'), may hold values from 0 to 31
- send_list: int32 [128, 8, 1024], P('grp', 'mem'), may hold values from 0 to 1023, each once within a row
- send_count: int32 [128, 8, 128], P('grp', 'mem'), may hold values from 1 to 8, as said below
Outputs:
- wave_out: float32 [2, 512, 256, 256], P(None, 'grp', 'mem')
- potential: float32 [256, 128, 128], P('grp', 'mem')
Inputs may be any that keep to these rules, and one draw needn't show every extreme that they name: `send_list`: each device's list names each of its 1024 beams once. `send_count`: every device fills all 8 slots toward some group.
All inputs are finite; a program needn't handle non-finite values.
Results may differ from a plain program's by a relative error of at most 0.0003.
Values sent between devices are 32-bit elements; how exact they have to be, the bound alone decides.
A program may use at most 64 MiB of HBM per device.

v0:
```python
import math

import jax
import jax.numpy as jnp
from jax import lax
from jax.sharding import Mesh
from jax.sharding import PartitionSpec as P

TILE = 16
CAP = 8
GRP = ("grp_0", "grp_1", "grp_2")


GRAV = 0.005
SCREEN = 0.0004
STEP_TIME = 0.2
HIGHEST = lax.Precision.HIGHEST


def in_blocks(x, dim, peers):
    lengths = x.shape
    tiles = x.reshape(*lengths[:dim], peers, lengths[dim] // peers, *lengths[dim + 1 :])
    return jnp.moveaxis(tiles, dim, 0)


def joined_along(tiles, dim):
    lengths = list(tiles.shape[1:])
    lengths[dim] *= tiles.shape[0]
    return jnp.moveaxis(tiles, 0, dim).reshape(lengths)


def exchange_in_order(tiles, axes, order):
    inside = tiles.shape[1:]
    filled = tiles.reshape(*(lax.axis_size(a) for a in axes), *inside)
    for k in order:
        filled = lax.all_to_all(filled, axes[k], k, k, tiled=True)
    return filled.reshape(-1, *inside)


def two_step_exchange(x, groups, order, split_dim, concat_dim):
    peers = lax.axis_size(groups[0]) * lax.axis_size(groups[1])
    tiles = in_blocks(x, split_dim, peers)
    return joined_along(exchange_in_order(tiles, groups, order), concat_dim)


def padded(block, sides, width):
    for axis, dim in sides:
        count = lax.axis_size(axis)
        forward = [(i, i + 1) for i in range(count - 1)]
        forward.append((count - 1, 0))
        backward = [(target, source) for source, target in forward]
        low = lax.ppermute(
            lax.slice_in_dim(block, block.shape[dim] - width, None, axis=dim), axis, forward
        )
        high = lax.ppermute(lax.slice_in_dim(block, 0, width, axis=dim), axis, backward)
        block = jnp.concatenate([low, block, high], axis=dim)
    return block


def profile(coords, centre, breadth, wavenum):
    offset = coords[None, :] - centre[:, None]
    envelope = jnp.exp(-(offset * offset) / (2.0 * breadth[:, None] * breadth[:, None]))
    phases = wavenum[:, None] * offset
    return (envelope * jnp.cos(phases), envelope * jnp.sin(phases))


def deposit(params, planes, columns, length):
    number = params.shape[1]
    z_real, z_imag = profile(
        jnp.arange(planes).astype(jnp.float32), params[0], params[8], params[3]
    )
    x_real, x_imag = profile(
        jnp.arange(columns).astype(jnp.float32), params[1], params[8], params[4]
    )
    y_real, y_imag = profile(
        jnp.arange(length).astype(jnp.float32), params[2], params[8], params[5]
    )
    amp_real = params[6][:, None]
    amp_imag = params[7][:, None]
    az_real = amp_real * z_real - amp_imag * z_imag
    az_imag = amp_real * z_imag + amp_imag * z_real
    left_real = (
        az_real[:, :, None] * x_real[:, None, :] - az_imag[:, :, None] * x_imag[:, None, :]
    ).reshape(number, planes * columns)
    left_imag = (
        az_real[:, :, None] * x_imag[:, None, :] + az_imag[:, :, None] * x_real[:, None, :]
    ).reshape(number, planes * columns)
    part_rr = jnp.einsum("bk,by->ky", left_real, y_real, precision=HIGHEST)
    part_ii = jnp.einsum("bk,by->ky", left_imag, y_imag, precision=HIGHEST)
    part_ri = jnp.einsum("bk,by->ky", left_real, y_imag, precision=HIGHEST)
    part_ir = jnp.einsum("bk,by->ky", left_imag, y_real, precision=HIGHEST)
    return jnp.stack([part_rr - part_ii, part_ri + part_ir]).reshape(2, planes, columns, length)


def centres(beam_offsets, beam_waves, beam_amps, beam_widths, beam_tile, planes, length):
    tiles_y = length // TILE
    tile_x = (beam_tile // tiles_y).astype(jnp.float32)
    tile_y = (beam_tile % tiles_y).astype(jnp.float32)
    centre_z = beam_offsets[0] * float(planes)
    centre_x = TILE * tile_x + TILE * beam_offsets[1]
    centre_y = TILE * tile_y + TILE * beam_offsets[2]
    return jnp.stack(
        [
            centre_z,
            centre_x,
            centre_y,
            beam_waves[0],
            beam_waves[1],
            beam_waves[2],
            beam_amps[0],
            beam_amps[1],
            beam_widths,
        ]
    )


def eigen_at(indices, number):
    return 2.0 * jnp.cos(2.0 * math.pi / number * indices.astype(jnp.float32)) - 2.0


def dft_tables(number):
    indices = jnp.arange(number, dtype=jnp.int32)
    turns = indices[:, None] * indices[None, :] % number
    angles = 2.0 * math.pi / number * turns.astype(jnp.float32)
    return (jnp.cos(angles), jnp.sin(angles))


def member_turn(stacked):
    return lax.all_to_all(stacked, "mem", split_axis=3, concat_axis=2, tiled=True)


def group_turn(stacked):
    return two_step_exchange(stacked, (("grp_0", "grp_1"), "grp_2"), (1, 0), 2, 1)


def solve_potential(coarse):
    planes_c = coarse.shape[0]
    length_y = coarse.shape[2]
    cos_y, sin_y = dft_tables(length_y)
    first_real = jnp.einsum("zxy,yk->zxk", coarse, cos_y, precision=HIGHEST)
    first_imag = -jnp.einsum("zxy,yk->zxk", coarse, sin_y, precision=HIGHEST)
    turned = member_turn(jnp.stack([first_real, first_imag]))
    full_x = turned.shape[2]
    part_y = turned.shape[3]
    cos_x, sin_x = dft_tables(full_x)
    second_real = jnp.einsum("zxy,xk->zky", turned[0], cos_x, precision=HIGHEST) + jnp.einsum(
        "zxy,xk->zky", turned[1], sin_x, precision=HIGHEST
    )
    second_imag = jnp.einsum("zxy,xk->zky", turned[1], cos_x, precision=HIGHEST) - jnp.einsum(
        "zxy,xk->zky", turned[0], sin_x, precision=HIGHEST
    )
    spun = group_turn(jnp.stack([second_real, second_imag]).reshape(2, planes_c, full_x * part_y))
    full_z = spun.shape[1]
    piece_len = spun.shape[2]
    cos_z, sin_z = dft_tables(full_z)
    third_real = jnp.einsum("zp,zk->pk", spun[0], cos_z, precision=HIGHEST) + jnp.einsum(
        "zp,zk->pk", spun[1], sin_z, precision=HIGHEST
    )
    third_imag = jnp.einsum("zp,zk->pk", spun[1], cos_z, precision=HIGHEST) - jnp.einsum(
        "zp,zk->pk", spun[0], sin_z, precision=HIGHEST
    )
    flat_index = lax.axis_index(GRP) * piece_len + jnp.arange(piece_len, dtype=jnp.int32)
    wave_x = flat_index // part_y
    wave_y = lax.axis_index("mem") * part_y + flat_index % part_y
    wave_z = jnp.arange(full_z, dtype=jnp.int32)
    eigenvalues = (
        eigen_at(wave_z, full_z)[None, :]
        + eigen_at(wave_x, full_x)[:, None]
        + eigen_at(wave_y, length_y)[:, None]
    )
    zero_mode = (wave_x == 0)[:, None] & (wave_y == 0)[:, None] & (wave_z == 0)[None, :]
    factor = jnp.where(zero_mode, 0.0, 1.0 / (eigenvalues - SCREEN))
    scaled_real = third_real * factor
    scaled_imag = third_imag * factor
    back_real = (
        jnp.einsum("pk,kz->pz", scaled_real, cos_z, precision=HIGHEST)
        - jnp.einsum("pk,kz->pz", scaled_imag, sin_z, precision=HIGHEST)
    ) / full_z
    back_imag = (
        jnp.einsum("pk,kz->pz", scaled_imag, cos_z, precision=HIGHEST)
        + jnp.einsum("pk,kz->pz", scaled_real, sin_z, precision=HIGHEST)
    ) / full_z
    returned = group_turn(jnp.stack([back_real, back_imag]))
    cube = returned.reshape(2, full_x, part_y, planes_c)
    fourth_real = (
        jnp.einsum("kyz,kx->zyx", cube[0], cos_x, precision=HIGHEST)
        - jnp.einsum("kyz,kx->zyx", cube[1], sin_x, precision=HIGHEST)
    ) / full_x
    fourth_imag = (
        jnp.einsum("kyz,kx->zyx", cube[1], cos_x, precision=HIGHEST)
        + jnp.einsum("kyz,kx->zyx", cube[0], sin_x, precision=HIGHEST)
    ) / full_x
    again = member_turn(jnp.stack([fourth_real, fourth_imag]))
    settled = (
        jnp.einsum("zkx,ky->zxy", again[0], cos_y, precision=HIGHEST)
        - jnp.einsum("zkx,ky->zxy", again[1], sin_y, precision=HIGHEST)
    ) / length_y
    return GRAV * settled


def drift_inner(extended, fine_pot):
    middle = extended[:, 1:-1, 1:-1]
    beside_all = (
        extended[:, :-2, 1:-1]
        + extended[:, 2:, 1:-1]
        + extended[:, 1:-1, :-2]
        + extended[:, 1:-1, 2:]
        + jnp.roll(middle, 1, 3)
        + jnp.roll(middle, -1, 3)
    )
    spread = beside_all - 6.0 * middle
    return jnp.stack(
        [-(0.5 * spread[1] - fine_pot * middle[1]), 0.5 * spread[0] - fine_pot * middle[0]]
    )


def crop(values, margin):
    return values[:, margin : values.shape[1] - margin, margin : values.shape[2] - margin]


def body(wave, beam_offsets, beam_waves, beam_amps, beam_widths, beam_tile, send_list, send_count):
    planes = wave.shape[1]
    columns = wave.shape[2]
    length = wave.shape[3]
    params = centres(
        beam_offsets[:, 0, 0],
        beam_waves[:, 0, 0],
        beam_amps[:, 0, 0],
        beam_widths[0, 0],
        beam_tile[0, 0],
        planes,
        length,
    )
    picked = jnp.take(params, send_list[0, 0], axis=1)
    groups_seen = send_count.shape[2]
    sent_mask = (
        (jnp.arange(CAP, dtype=jnp.int32)[None, :] < send_count[0, 0][:, None])
        .astype(jnp.float32)
        .reshape(groups_seen * CAP)
    )
    picked = jnp.concatenate([picked[:6], picked[6:8] * sent_mask[None], picked[8:]], axis=0)
    arrived = lax.all_to_all(picked, GRP, split_axis=1, concat_axis=1, tiled=True)
    field_now = wave + deposit(arrived, planes, columns, length)
    density = field_now[0] * field_now[0] + field_now[1] * field_now[1]
    coarse = density.reshape(planes // 2, 2, columns // 2, 2, length // 2, 2).mean(axis=(1, 3, 5))
    potential = solve_potential(coarse)
    fine_pot = jnp.repeat(jnp.repeat(jnp.repeat(potential, 2, 0), 2, 1), 2, 2)
    extended = padded(
        jnp.concatenate([field_now, fine_pot[None]], axis=0), ((GRP, 1), ("mem", 2)), 4
    )
    start = extended[:2]
    pot_wide = extended[2:3]
    slope_one = drift_inner(start, crop(pot_wide, 1)[0])
    slope_two = drift_inner(crop(start, 1) + 0.5 * STEP_TIME * slope_one, crop(pot_wide, 2)[0])
    slope_three = drift_inner(crop(start, 2) + 0.5 * STEP_TIME * slope_two, crop(pot_wide, 3)[0])
    slope_four = drift_inner(crop(start, 3) + STEP_TIME * slope_three, crop(pot_wide, 4)[0])
    field_now = crop(start, 4) + STEP_TIME / 6.0 * (
        crop(slope_one, 3) + 2.0 * crop(slope_two, 2) + 2.0 * crop(slope_three, 1) + slope_four
    )
    return (field_now, potential)


def solution(mesh):
    split = Mesh(
        mesh.devices.reshape(8, 8, 2, mesh.shape["mem"]), ("grp_0", "grp_1", "grp_2", "mem")
    )
    in_specs = (
        P(None, GRP, "mem", None),
        P(None, GRP, "mem", None),
        P(None, GRP, "mem", None),
        P(None, GRP, "mem", None),
        P(GRP, "mem", None),
        P(GRP, "mem", None),
        P(GRP, "mem", None),
        P(GRP, "mem", None),
    )
    out_specs = (P(None, GRP, "mem", None), P(GRP, "mem", None))
    return jax.shard_map(body, mesh=split, in_specs=in_specs, out_specs=out_specs, check_vma=False)
```

profile of v0, /device:TPU:14, one launch (start us, length us, event | category | flops | bytes accessed | tf_op | source)
XLA Modules:
  0.0 215.3 jit_solution(15969485319847918227)
XLA Ops:
  1.3 0.8 fusion.157
  2.1 0.8 slice_bitcast_fusion.6
  2.8 0.8 stack.71
  5.2 0.7 fusion.124
  6.1 2.8 %gather_fusion = f32[1024,9]{1,0:T(8,128)S(1)} fusion(f32[9,1024]{0,1:T(8,128)S(1)} %copy.296, s32[1024]{0:T(1024)S(1)} %broadcast_clamp_fusion), kind=kCustom, calls=%fused_computation | custom fusion | bytes 77824 | tf_op jit(solution)/shard_map/jit(_take)/gather | solution.py:234
  9.6 1.1 maximum_bitcast_fusion
  10.8 24.8 %all-to-all-start = ((f32[9,128,8]{0,2,1:T(8,128)}), f32[9,128,8]{0,2,1:T(8,128)S(1)}, u32[]{:S(2)}, u32[]{:S(2)}) async-start(f32[9,128,8]{0,2,1:T(8,128)} %maximum_bitcast_fusion), calls=%async_computation | async-start | bytes 1048576 | tf_op jit(solution)/shard_map/all_to_all | solution.py:242
  35.7 19.1 %all-to-all-done = f32[9,128,8]{0,2,1:T(8,128)S(1)} async-done(((f32[9,128,8]{0,2,1:T(8,128)}), f32[9,128,8]{0,2,1:T(8,128)S(1)}, u32[]{:S(2)}, u32[]{:S(2)}) %all-to-all-start) | async-done | bytes 36896 | tf_op jit(solution)/shard_map/all_to_all | solution.py:242
  54.8 2.4 %slice_reduce_fusion.1 = (f32[128,8]{1,0:T(8,128)S(1)}, f32[128,8]{1,0:T(8,128)S(1)}, f32[128,8]{1,0:T(8,128)S(1)}, f32[128,8]{1,0:T(8,128)S(1)}, f32[128,8]{1,0...) fusion(f32[9,128,8]{0,2,1:T(8,128)S(1)} %all-to-all-done), kind=kLoop, calls=%fused_computation.61 | loop fusion | bytes 73728 | tf_op jit(solution)/shard_map/slice | solution.py:76
  59.0 4.4 %fusion.26 = f32[128,256]{1,0:T(8,128)S(1)} fusion(f32[1024,128]{0,1:T(8,128)S(1)} %bitcast.210, f32[1024]{0:T(1024)S(1)} %mul.687, f32[1024]{0:T(1024)S(1)} %sub.175, f32[256]{0:T(256)S(1)} %iota_convert_fusion, f32[1024]{0:T(1024)S(1)} %multiply_multiply_fusion), kind=kOutput, calls=%fused_computation.44 | convolution fusion | flops 404226048 | bytes 668672 | tf_op jit(solution)/shard_map/bk,by->ky/dot_general | solution.py:88
  63.4 4.8 %fusion.22 = f32[128,256]{1,0:T(8,128)S(1)} fusion(f32[1024,128]{0,1:T(8,128)S(1)} %bitcast.211, f32[1024]{0:T(1024)S(1)} %mul.687, f32[1024]{0:T(1024)S(1)} %sub.175, f32[256]{0:T(256)S(1)} %iota_convert_fusion, f32[1024]{0:T(1024)S(1)} %multiply_multiply_fusion), kind=kOutput, calls=%fused_computation.43 | convolution fusion | flops 404226048 | bytes 668672 | tf_op jit(solution)/shard_map/bk,by->ky/dot_general | solution.py:90
  68.2 4.4 %convolution_subtract_fusion = f32[128,256]{1,0:T(8,128)S(1)} fusion(f32[128,256]{1,0:T(8,128)S(1)} %fusion.26, f32[1024,128]{0,1:T(8,128)S(1)} %bitcast.208, f32[1024]{0:T(1024)S(1)} %mul.687, f32[1024]{0:T(1024)S(1)} %sub.175, f32[256]{0:T(256)S(1)} %iota_convert_fusion, f32[1024]{0:T(1024)S(1)} %multiply_multiply_fusion), kind=kOutput, calls=%fused_computation.7 | convolution fusion | flops 404258816 | bytes 799744 | tf_op jit(solution)/shard_map/bk,by->ky/dot_general | solution.py:89
  72.7 4.4 %convolution_add_fusion = f32[128,256]{1,0:T(8,128)S(1)} fusion(f32[128,256]{1,0:T(8,128)S(1)} %fusion.22, f32[1024,128]{0,1:T(8,128)S(1)} %bitcast.209, f32[1024]{0:T(1024)S(1)} %mul.687, f32[1024]{0:T(1024)S(1)} %sub.175, f32[256]{0:T(256)S(1)} %iota_convert_fusion, f32[1024]{0:T(1024)S(1)} %multiply_multiply_fusion), kind=kOutput, calls=%fused_computation.6 | convolution fusion | flops 404258816 | bytes 799744 | tf_op jit(solution)/shard_map/bk,by->ky/dot_general | solution.py:91
  77.2 9.7 %add.349 = f32[2,2,16,2,128,2]{5,4,3,2,1,0:T(8,128)} reshape(f32[1,4,32,256]{3,2,1,0:T(8,128)S(1)} %fusion.92) | data formatting | bytes 262144 | tf_op jit(solution)/shard_map/add | solution.py:244
  86.9 4.0 %reduce_sum.9 = f32[2,16,128]{2,1,0:T(8,128)S(1)} reduce(f32[2,2,16,2,128,2]{5,4,3,2,1,0:T(8,128)} %add.349, f32[]{:T(128)} %constant.148.clone.1), dimensions={1,3,5}, to_apply=%region_0.1 | reduce | flops 28672 | bytes 147460 | tf_op jit(solution)/shard_map/reduce_sum | solution.py:245
  92.0 0.9 reshape.734
  92.9 7.1 %all-to-all-start.1 = ((f32[8,1,1024]{2,1,0:T(1,128)}), f32[8,1,1024]{2,1,0:T(1,128)S(1)}, u32[]{:S(2)}, u32[]{:S(2)}) async-start(f32[8,1,1024]{2,1,0:T(1,128)} %reshape.734), calls=%async_computation.1 | async-start | bytes 65536 | tf_op jit(solution)/shard_map/all_to_all | solution.py:129
  100.1 5.2 %all-to-all-done.1 = f32[8,1,1024]{2,1,0:T(1,128)S(1)} async-done(((f32[8,1,1024]{2,1,0:T(1,128)}), f32[8,1,1024]{2,1,0:T(1,128)S(1)}, u32[]{:S(2)}, u32[]{:S(2)}) %all-to-all-start.1) | async-done | bytes 32800 | tf_op jit(solution)/shard_map/all_to_all | solution.py:129
  105.7 0.7 reduce.18
  109.4 3.7 %all_to_all.59 = f32[2,1,4096]{2,1,0:T(1,128)S(1)} all-to-all(f32[2,1,4096]{2,1,0:T(1,128)S(1)} %reshape.736), channel_id=1, replica_groups=mesh['grp_0'=8,'grp_1'=8,'grp_2'=2,'mem'=8] {'grp_2'}, dimensions={0} | all-to-all | bytes 65536 | tf_op jit(solution)/shard_map/all_to_all | solution.py:36
  113.1 0.7 reduce.19
  114.2 0.9 reshape.738
  115.2 5.5 %all-to-all-start.3 = ((f32[64,1,128]{2,1,0:T(1,128)}), f32[64,1,128]{2,1,0:T(1,128)S(1)}, u32[]{:S(2)}, u32[]{:S(2)}) async-start(f32[64,1,128]{2,1,0:T(1,128)} %reshape.738), calls=%async_computation.3 | async-start | bytes 65536 | tf_op jit(solution)/shard_map/all_to_all | solution.py:36
  120.7 12.0 %all-to-all-done.3 = f32[64,1,128]{2,1,0:T(1,128)S(1)} async-done(((f32[64,1,128]{2,1,0:T(1,128)}), f32[64,1,128]{2,1,0:T(1,128)S(1)}, u32[]{:S(2)}, u32[]{:S(2)}) %all-to-all-start.3) | async-done | bytes 32800 | tf_op jit(solution)/shard_map/all_to_all | solution.py:36
  132.7 0.7 reduce.20
  134.0 1.2 fusion.101
  135.4 1.2 fusion.97
  136.5 1.2 fusion.11
  137.8 1.2 fusion.99
  138.9 1.2 fusion.10
  140.2 1.2 fusion.95
  141.4 1.2 fusion.8
  142.8 1.2 fusion.7
  144.6 3.7 %all_to_all.60 = f32[2,1,4096]{2,1,0:T(1,128)S(1)} all-to-all(f32[2,1,4096]{2,1,0:T(1,128)S(1)} %reshape.740), channel_id=1, replica_groups=mesh['grp_0'=8,'grp_1'=8,'grp_2'=2,'mem'=8] {'grp_2'}, dimensions={0} | all-to-all | bytes 65536 | tf_op jit(solution)/shard_map/all_to_all | solution.py:36
  148.3 0.7 reduce.21
  149.7 16.1 %all_to_all.61 = f32[64,1,128]{2,1,0:T(1,128)S(1)} all-to-all(f32[64,1,128]{2,1,0:T(1,128)S(1)} %reshape.742), channel_id=1, replica_groups=mesh['grp_0'=8,'grp_1'=8,'grp_2'=2,'mem'=8] {'grp_0','grp_1'}, dimensions={0} | all-to-all | bytes 65536 | tf_op jit(solution)/shard_map/all_to_all | solution.py:36
  165.9 0.7 reduce.22
  169.5 10.4 %all_to_all.62 = f32[8,1,1024]{2,1,0:T(1,128)S(1)} all-to-all(f32[8,1,1024]{2,1,0:T(1,128)S(1)} %reshape.744), channel_id=1, replica_groups=mesh['grp_0'=8,'grp_1'=8,'grp_2'=2,'mem'=8] {'mem'}, dimensions={0} | all-to-all | bytes 65536 | tf_op jit(solution)/shard_map/all_to_all | solution.py:129
  179.9 0.7 reduce.23
  182.8 1.9 collective-permute-start
  184.7 7.0 %collective-permute-start.1 = (f32[3,4,32,256]{3,2,1,0:T(8,128)S(1)}, f32[3,4,32,256]{3,2,1,0:T(8,128)S(1)}, u32[]{:S(2)}, u32[]{:S(2)}) collective-permute-start(f32[3,4,32,256]{3,2,1,0:T(8,128)S(1)} %pad_maximum_fusion.4), channel_id=1, source_target_pairs={{8,0},{16,8},{24,16},{32,24},{40,32},{48,40},{56,48},{64,56},{72,6... | collective-permute-start | bytes 1179656 | tf_op jit(solution)/shard_map/ppermute | solution.py:55
  191.7 3.5 %collective-permute-done = f32[3,4,32,256]{3,2,1,0:T(8,128)S(1)} collective-permute-done((f32[3,4,32,256]{3,2,1,0:T(8,128)S(1)}, f32[3,4,32,256]{3,2,1,0:T(8,128)S(1)}, u32[]{:S(2)}, u32[]{:S(2)}) %collective-permute-start) | collective-permute-done | bytes 393248 | tf_op jit(solution)/shard_map/ppermute | solution.py:52
  195.2 1.8 collective-permute-done.1
  197.1 4.8 %collective-permute-start.2 = (f32[3,12,4,256]{3,2,1,0:T(4,128)S(1)}, f32[3,12,4,256]{3,2,1,0:T(4,128)S(1)}, u32[]{:S(2)}, u32[]{:S(2)}) collective-permute-start(f32[3,12,4,256]{3,2,1,0:T(4,128)S(1)} %get-tuple-element.29), channel_id=1, source_target_pairs={{0,1},{1,2},{2,3},{3,4},{4,5},{5,6},{6,7},{7,0},{8,9},{9,10},{10,1... | collective-permute-start | bytes 442376 | tf_op jit(solution)/shard_map/ppermute | solution.py:52
  201.8 1.9 collective-permute-start.3
  203.8 0.7 collective-permute-done.2
  204.5 5.6 %collective-permute-done.3 = f32[3,12,4,256]{3,2,1,0:T(4,128)S(1)} collective-permute-done((f32[3,12,4,256]{3,2,1,0:T(4,128)S(1)}, f32[3,12,4,256]{3,2,1,0:T(4,128)S(1)}, u32[]{:S(2)}, u32[]{:S(2)}) %collective-permute-start.3) | collective-permute-done | bytes 147488 | tf_op jit(solution)/shard_map/ppermute | solution.py:55
  214.1 0.9 fusion.68
  (117 shorter events, 20.8 us)
Async XLA Ops:
  10.8 44.1 %all-to-all-start = ((f32[9,128,8]{0,2,1:T(8,128)}), f32[9,128,8]{0,2,1:T(8,128)S(1)}, u32[]{:S(2)}, u32[]{:S(2)}) async-start(f32[9,128,8]{0,2,1:T(8,128)} %maximum_bitcast_fusion), calls=%async_computation | async-start | bytes 1048576 | tf_op jit(solution)/shard_map/all_to_all | solution.py:242
  72.7 4.4 %copy-start = (f32[2,4,32,256]{3,2,1,0:T(8,128)S(1)}, f32[2,4,32,256]{3,2,1,0:T(8,128)}, u32[]{:S(2)}) copy-start(f32[2,4,32,256]{3,2,1,0:T(8,128)} %param.8) | copy-start | bytes 786436
  92.9 12.3 %all-to-all-start.1 = ((f32[8,1,1024]{2,1,0:T(1,128)}), f32[8,1,1024]{2,1,0:T(1,128)S(1)}, u32[]{:S(2)}, u32[]{:S(2)}) async-start(f32[8,1,1024]{2,1,0:T(1,128)} %reshape.734), calls=%async_computation.1 | async-start | bytes 65536 | tf_op jit(solution)/shard_map/all_to_all | solution.py:129
  115.2 17.5 %all-to-all-start.3 = ((f32[64,1,128]{2,1,0:T(1,128)}), f32[64,1,128]{2,1,0:T(1,128)S(1)}, u32[]{:S(2)}, u32[]{:S(2)}) async-start(f32[64,1,128]{2,1,0:T(1,128)} %reshape.738), calls=%async_computation.3 | async-start | bytes 65536 | tf_op jit(solution)/shard_map/all_to_all | solution.py:36
  182.2 14.8 %copy-start.1 = (f32[2,16,128]{2,1,0:T(8,128)}, f32[2,16,128]{2,1,0:T(8,128)S(1)}, u32[]{:S(2)}) copy-start(f32[2,16,128]{2,1,0:T(8,128)S(1)} %fusion.2) | copy-start | bytes 49156
  182.8 12.4 %collective-permute-start = (f32[3,4,32,256]{3,2,1,0:T(8,128)S(1)}, f32[3,4,32,256]{3,2,1,0:T(8,128)S(1)}, u32[]{:S(2)}, u32[]{:S(2)}) collective-permute-start(f32[3,4,32,256]{3,2,1,0:T(8,128)S(1)} %pad_maximum_fusion.4), channel_id=1, source_target_pairs={{0,8},{8,16},{16,24},{24,32},{32,40},{40,48},{48,56},{56,64},{64,7... | collective-permute-start | bytes 1179656 | tf_op jit(solution)/shard_map/ppermute | solution.py:52
  184.7 12.2 %collective-permute-start.1 = (f32[3,4,32,256]{3,2,1,0:T(8,128)S(1)}, f32[3,4,32,256]{3,2,1,0:T(8,128)S(1)}, u32[]{:S(2)}, u32[]{:S(2)}) collective-permute-start(f32[3,4,32,256]{3,2,1,0:T(8,128)S(1)} %pad_maximum_fusion.4), channel_id=1, source_target_pairs={{8,0},{16,8},{24,16},{32,24},{40,32},{48,40},{56,48},{64,56},{72,6... | collective-permute-start | bytes 1179656 | tf_op jit(solution)/shard_map/ppermute | solution.py:55
  197.1 7.4 %collective-permute-start.2 = (f32[3,12,4,256]{3,2,1,0:T(4,128)S(1)}, f32[3,12,4,256]{3,2,1,0:T(4,128)S(1)}, u32[]{:S(2)}, u32[]{:S(2)}) collective-permute-start(f32[3,12,4,256]{3,2,1,0:T(4,128)S(1)} %get-tuple-element.29), channel_id=1, source_target_pairs={{0,1},{1,2},{2,3},{3,4},{4,5},{5,6},{6,7},{7,0},{8,9},{9,10},{10,1... | collective-permute-start | bytes 442376 | tf_op jit(solution)/shard_map/ppermute | solution.py:52
  201.8 8.2 %collective-permute-start.3 = (f32[3,12,4,256]{3,2,1,0:T(4,128)S(1)}, f32[3,12,4,256]{3,2,1,0:T(4,128)S(1)}, u32[]{:S(2)}, u32[]{:S(2)}) collective-permute-start(f32[3,12,4,256]{3,2,1,0:T(4,128)S(1)} %get-tuple-element.30), channel_id=1, source_target_pairs={{1,0},{2,1},{3,2},{4,3},{5,4},{6,5},{7,6},{0,7},{9,8},{10,9},{11,1... | collective-permute-start | bytes 442376 | tf_op jit(solution)/shard_map/ppermute | solution.py:55
where the time goes:
time: 219 us; the launch traced here: 215 us
  starting transfers between devices  53 us (24%)
  waiting for transfers between devices  47.9 us (22%)
  blocking collectives  34 us (16%)
  matrix products  32.7 us (15%)
  local copies, waits for them, and re-layouts  27.7 us (13%)
  other arithmetic  18.3 us (8%)
    all_to_all x1, starting transfers between devices, body(): lax.all_to_all(picked, GRP, split_axis=1, concat_axis=1, tiled=True)  24.8 us
    all_to_all x3, blocking collectives, exchange_in_order(): filled = lax.all_to_all(filled, axes[k], k, k, tiled=True)  23.6 us
    all_to_all x1, waiting for transfers between devices, body(): lax.all_to_all(picked, GRP, split_axis=1, concat_axis=1, tiled=True)  19.1 us
    all_to_all x1, waiting for transfers between devices, exchange_in_order(): filled = lax.all_to_all(filled, axes[k], k, k, tiled=True)  12 us
    all_to_all x1, blocking collectives, member_turn(): lax.all_to_all(stacked, 'mem', split_axis=3, concat_axis=2, tiled=True)  10.4 us
    add x1, local copies, waits for them, and re-layouts, body(): density = field_now[0] * field_now[0] + field_now[1] * field_now[1]  9.74 us
    ppermute x2, starting transfers between devices, padded(): lax.ppermute(lax.slice_in_dim(block, 0, width, axis=dim), axis, backward)  8.88 us
    ppermute x2, waiting for transfers between devices, padded(): lax.ppermute(lax.slice_in_dim(block, 0, width, axis=dim), axis, backward)  7.35 us
  transfers between devices with their start and end apart: 7, of which 7 were waited for; matrix products, arithmetic and copies ran while one was open for 0% of the time, Pallas kernels for 0%

commit v1 on v0

v1 whole, which is shorter than its diff:
```python
import functools
import math

import jax
import jax.numpy as jnp
import numpy as np
from jax import lax
from jax.experimental import pallas as pl
from jax.experimental.pallas import tpu as pltpu
from jax.sharding import PartitionSpec as P


F32 = jnp.float32
BF16 = jnp.bfloat16
HIGHEST = lax.Precision.HIGHEST
MESH = pl.DeviceIdType.MESH

GRAV = 0.005
SCREEN = 0.0004
STEP_TIME = 0.2

G = 128
M = 8
SLOTS = 8
PLANES = 4
COLS = 32
NY = 256
BEAMS = 1024
PAD = 8
EXT_Z = PLANES + 8
EXT_X = COLS + 2 * PAD
PLANE_ROWS = ((0, 0, 24), (1, 24, 24), (-1, 48, 24), (2, 72, 24), (-2, 96, 16), (3, 112, 16))


def basis(number):
    half = number // 2
    at = np.arange(number)
    waves = np.concatenate([np.arange(half + 1), np.arange(1, half)])
    angles = 2.0 * np.pi / number * (waves[:, None] * at[None, :] % number)
    vectors = np.where(np.arange(number)[:, None] <= half, np.cos(angles), np.sin(angles))
    return vectors, (vectors**2).sum(1), 2.0 * np.cos(2.0 * np.pi / number * waves) - 2.0


@functools.cache
def tables():
    vec_y, len_y, eig_y = basis(128)
    vec_x, len_x, eig_x = vec_y, len_y, eig_y
    wz = np.arange(128)
    at = np.arange(256)
    ang = 2.0 * np.pi / 256 * (wz[:, None] * at[None, :] % 256)
    second = np.sin(ang)
    second[0] = np.cos(np.pi * at)
    vec_z = np.concatenate([np.cos(ang), second])
    len_z = (vec_z**2).sum(1)
    lam = 2.0 * np.cos(2.0 * np.pi / 256 * wz) - 2.0
    lam_second = lam.copy()
    lam_second[0] = -4.0
    eig_z = np.concatenate([lam, lam_second])

    fwd_y = np.repeat(vec_y, 2, axis=1)
    fwd_z = np.concatenate([vec_z[:, 0::2], vec_z[:, 1::2]], axis=1).T
    fwd_x = vec_x
    inv_x = np.zeros((128, 128))
    shift = np.zeros(128)
    for offset, first, rows in PLANE_ROWS:
        margin = (rows - 16) // 2
        where = (np.arange(rows) - margin) % 128
        inv_x[first : first + rows] = (vec_x / len_x[:, None])[:, where].T
        shift[first : first + rows] = offset
    turn = 2.0 * np.pi / 256 * wz[None, :] * shift[:, None]
    rot_c, rot_s = np.cos(turn), np.sin(turn)
    rot_d = rot_c.copy()
    rot_d[:, 0] = np.cos(np.pi * shift)
    inv_z = (vec_z / len_z[:, None])[:, 0::2].T
    inv_y = (vec_y / len_y[:, None]).copy()
    inv_y = np.concatenate([np.repeat(inv_y, 2, axis=1), inv_y], axis=1)
    lam_xz = eig_x[:, None] + eig_z[None, :] - SCREEN
    lam_y = np.broadcast_to(eig_y[:, None, None], (128, 1, 256))
    many = (fwd_y, fwd_z, fwd_x, inv_x, rot_c, rot_s, rot_d, inv_z, inv_y, lam_xz, lam_y)
    return tuple(np.ascontiguousarray(t, dtype=np.float32) for t in many)


SIN = tuple((-1.0) ** i / math.factorial(2 * i + 1) for i in range(6))
COS = tuple((-1.0) ** i / math.factorial(2 * i) for i in range(7))
TURN_HIGH = 6.28125
TURN_LOW = 2.0 * math.pi - TURN_HIGH


def cos_sin(phase):
    turns = jnp.round(phase * (0.5 / math.pi))
    half = 0.5 * ((phase - turns * TURN_HIGH) - turns * TURN_LOW)
    square = half * half
    sine = SIN[-1]
    for c in SIN[-2::-1]:
        sine = sine * square + c
    sine = sine * half
    cosine = COS[-1]
    for c in COS[-2::-1]:
        cosine = cosine * square + c
    return 1.0 - 2.0 * (sine * sine), 2.0 * (sine * cosine)


def parts(value):
    high = value.astype(BF16)
    return high, (value - high.astype(F32)).astype(BF16)


def dot(a, b):
    return jnp.dot(a, b, precision=HIGHEST, preferred_element_type=F32)


def dot_t(a, b, precision=HIGHEST):
    dims = (((1,), (1,)), ((), ()))
    return lax.dot_general(a, b, dims, precision=precision, preferred_element_type=F32)


def iota(shape, dim):
    return lax.broadcasted_iota(jnp.int32, shape, dim)


N_TAB = 11
TAB_SHAPES = (
    (128, 256), (256, 256), (128, 128), (128, 128), (128, 128), (128, 128), (128, 128),
    (128, 256), (128, 384), (128, 256), (1, 256),
)
ARG_SHAPES = (
    ((2, PLANES, COLS, NY), F32), ((3, 1, BEAMS), F32), ((3, 1, BEAMS), F32), ((2, 1, BEAMS), F32),
    ((1, BEAMS), F32), ((1, BEAMS), jnp.int32), ((1, BEAMS), jnp.int32), ((1, G), jnp.int32),
)
N_ARG = len(ARG_SHAPES)


def kernel(*refs):
    args_hbm, refs = refs[:N_ARG], refs[N_ARG:]
    tabs_hbm, refs = refs[:N_TAB], refs[N_TAB:]
    wave_out, pot_out = refs[:2]
    refs = refs[2:]
    args_v, refs = refs[:N_ARG], refs[N_ARG:]
    tabs_v, refs = refs[:N_TAB], refs[N_TAB:]
    (
        rows_v, one_v, two_v, send1, recv1, send2, recv2, send3, recv3, own_x, all_x,
        left_h, left_l, right_h, right_l, dens_v, pot_v, field_a, field_b, out_v, pot_c,
        arg_sem, tab_sem, out_sem, s_sem, r_sem, xs_sem, xr_sem, hs_sem, hr_sem,
    ) = refs
    wave_v, off_v, wav_v, amp_v, wid_v, til_v, sl_v, cnt_v = args_v
    (fwd_y, fwd_z, fwd_x, inv_x, rot_c, rot_s, rot_d, inv_z, inv_y, lam_xz, lam_y) = tabs_v

    g = lax.axis_index("grp")
    m = lax.axis_index("mem")
    barrier = pltpu.get_barrier_semaphore()

    def greet(j, carry):
        pl.semaphore_signal(
            barrier, inc=1, device_id=(lax.rem(g + j, G), m), device_id_type=MESH
        )
        return carry

    lax.fori_loop(1, G, greet, 0)
    for j in range(1, M):
        pl.semaphore_signal(
            barrier, inc=1, device_id=(g, lax.rem(m + j, M)), device_id_type=MESH
        )
    up, down = lax.rem(g + 1, G), lax.rem(g + G - 1, G)
    right, left = lax.rem(m + 1, M), lax.rem(m + M - 1, M)
    for corner in ((up, right), (up, left), (down, right), (down, left)):
        pl.semaphore_signal(barrier, inc=1, device_id=corner, device_id_type=MESH)

    arg_copies = [
        pltpu.make_async_copy(args_hbm[i], args_v[i], arg_sem.at[i]) for i in range(N_ARG)
    ]
    for i in (6, 5, 1, 2, 3, 4, 7, 0):
        arg_copies[i].start()
    tab_copies = []
    for i in range(N_TAB):
        source = tabs_hbm[i].at[g] if i == N_TAB - 1 else tabs_hbm[i]
        tab_copies.append(pltpu.make_async_copy(source, tabs_v[i], tab_sem.at[i]))
        tab_copies[i].start()

    arg_copies[6].wait()
    listed = jnp.broadcast_to(sl_v[...], (SLOTS, BEAMS))
    mine = (iota((SLOTS, BEAMS), 1) & (SLOTS - 1)) == iota((SLOTS, BEAMS), 0)
    listed = jnp.concatenate(
        [jnp.where(mine, listed >> 5, 0), jnp.where(mine, listed & 31, 0)], axis=0
    )
    spread = (iota((BEAMS, G), 0) >> 3) == iota((BEAMS, G), 1)
    found = jnp.dot(
        listed.astype(F32).astype(BF16),
        jnp.where(spread, 1.0, 0.0).astype(BF16),
        preferred_element_type=F32,
    )
    by_slot = (found[:SLOTS] * 32.0 + found[SLOTS:]).astype(jnp.int32)

    for i in (1, 2, 3, 4, 5, 7):
        arg_copies[i].wait()
    tile = til_v[...]
    rows_v[...] = jnp.zeros_like(rows_v)
    rows_v[0:1, :] = off_v[0] * float(PLANES)
    rows_v[1:2, :] = 16.0 * (tile >> 4).astype(F32) + 16.0 * off_v[1]
    rows_v[2:3, :] = 16.0 * (tile & 15).astype(F32) + 16.0 * off_v[2]
    for d in range(3):
        rows_v[3 + d : 4 + d, :] = wav_v[d]
    rows_v[6:7, :] = amp_v[0]
    rows_v[7:8, :] = amp_v[1]
    rows_v[8:9, :] = wid_v[...]
    exact = rows_v[...]
    first, rest = parts(exact)
    second = rest
    third = ((exact - first.astype(F32)) - second.astype(F32)).astype(BF16)
    three = jnp.concatenate([first, second, third], axis=0)
    for c in range(SLOTS):
        chosen = iota((BEAMS, G), 0) == by_slot[c : c + 1, :]
        picked = jnp.dot(
            three, jnp.where(chosen, 1.0, 0.0).astype(BF16), preferred_element_type=F32
        )
        one_v[pl.ds(c, 16, stride=SLOTS), :] = picked[0:16] + picked[16:32] + picked[32:48]
    filled = iota((SLOTS, G), 0) < cnt_v[...]
    for p in (6, 7):
        rows = slice(p * SLOTS, (p + 1) * SLOTS)
        one_v[rows, :] = jnp.where(filled, one_v[rows, :], 0.0)
    send1[:, 0, :] = one_v[...].T

    pl.semaphore_wait(barrier, (G - 1) + (M - 1) + 4)

    def scatter(source, target, number):
        def one(j, carry):
            h = lax.rem(g + j, G)
            pltpu.make_async_remote_copy(
                src_ref=source.at[h],
                dst_ref=target.at[g],
                send_sem=s_sem.at[number],
                recv_sem=r_sem.at[number],
                device_id=(h, m),
                device_id_type=MESH,
            ).start()
            return carry

        lax.fori_loop(1, G, one, 0)
        target[g] = source[g]

    def others(ref):
        return ref.at[pl.ds(0, G - 1)]

    def arrived(target, number):
        pltpu.make_async_copy(others(target), others(target), r_sem.at[number]).wait()

    def left_behind(source, number):
        pltpu.make_async_copy(others(source), others(source), s_sem.at[number]).wait()

    scatter(send1, recv1, 0)
    arrived(recv1, 0)

    two_v[...] = recv1[:, 0, :].T

    def profiles(c, carry):
        def row(p):
            return two_v[pl.ds(p * SLOTS + c, 1), :]

        width = row(8)
        scale = -0.5 / (width * width)
        at = pl.multiple_of(c * 256, 256)
        low, high = pl.ds(at, 128), pl.ds(at + 128, 128)

        away = iota((8, G), 0).astype(F32) - row(0)
        bell = jnp.exp(away * away * scale)
        cosine, sine = cos_sin(row(3) * away)
        z_r, z_i = bell * cosine, bell * sine
        a_r, a_i = row(6), row(7)
        az_r, az_i = a_r * z_r - a_i * z_i, a_r * z_i + a_i * z_r

        away = iota((COLS, G), 0).astype(F32) - row(1)
        bell = jnp.exp(away * away * scale)
        cosine, sine = cos_sin(row(4) * away)
        x_r, x_i = bell * cosine, bell * sine
        for z in range(PLANES):
            p_r, p_i = az_r[z : z + 1], az_i[z : z + 1]
            real, imag = p_r * x_r - p_i * x_i, p_r * x_i + p_i * x_r
            real_h, real_l = parts(real)
            imag_h, imag_l = parts(imag)
            top = slice(z * COLS, (z + 1) * COLS)
            bottom = slice(128 + z * COLS, 128 + (z + 1) * COLS)
            left_h[top, low] = real_h
            left_l[top, low] = real_l
            left_h[top, high] = -imag_h
            left_l[top, high] = -imag_l
            left_h[bottom, low] = imag_h
            left_l[bottom, low] = imag_l
            left_h[bottom, high] = real_h
            left_l[bottom, high] = real_l

        c_y, k_y = row(2), row(5)
        step = iota((16, G), 0).astype(F32)
        coarse_c, coarse_s = cos_sin(k_y * (16.0 * step - c_y))
        fine_c, fine_s = cos_sin(k_y * step)
        for a in range(16):
            away = (step + 16.0 * a) - c_y
            bell = jnp.exp(away * away * scale)
            b_c, b_s = coarse_c[a : a + 1], coarse_s[a : a + 1]
            real_h, real_l = parts(bell * (b_c * fine_c - b_s * fine_s))
            imag_h, imag_l = parts(bell * (b_s * fine_c + b_c * fine_s))
            rows = slice(16 * a, 16 * a + 16)
            right_h[rows, low] = real_h
            right_l[rows, low] = real_l
            right_h[rows, high] = imag_h
            right_l[rows, high] = imag_l
        return carry

    lax.fori_loop(0, SLOTS, profiles, 0)
    deposited = (
        dot_t(left_h[...], right_h[...], None)
        + dot_t(left_l[...], right_h[...], None)
        + dot_t(left_h[...], right_l[...], None)
    )
    arg_copies[0].wait()
    own_z, own_cols = pl.ds(4, PLANES), pl.ds(PAD, COLS)
    for z in range(PLANES):
        for part in range(2):
            rows = slice(part * 128 + z * COLS, part * 128 + (z + 1) * COLS)
            field_a[part, 4 + z, own_cols, :] = wave_v[part, z] + deposited[rows]
    for z in range(2):
        total = None
        for plane in (4 + 2 * z, 5 + 2 * z):
            for part in range(2):
                value = field_a[part, plane, own_cols, :]
                total = value * value if total is None else total + value * value
        for side in range(2):
            dens_v[side, z * COLS : (z + 1) * COLS, :] = total[:, side * 128 : (side + 1) * 128]
    pooled = [
        dens_v[side, pl.ds(0, COLS, stride=2), :] + dens_v[side, pl.ds(1, COLS, stride=2), :]
        for side in range(2)
    ]
    pooled = jnp.concatenate(pooled, axis=1)

    for copy in tab_copies:
        copy.wait()
    pooled = jnp.concatenate([pooled, jnp.zeros((96, NY), F32)], axis=0)
    send2[:, 0, :] = dot_t(fwd_y[...], pooled)
    scatter(send2, recv2, 1)

    first_cols, last_cols = pl.ds(PAD, 8), pl.ds(PAD + COLS - 8, 8)
    low_cols, high_cols = pl.ds(0, 8), pl.ds(PAD + COLS, 8)
    low_z, high_z = pl.ds(0, 4), pl.ds(8, 4)
    margin = []
    for i, (who, there_z, here_x, there_x) in enumerate(
        (
            ((up, m), low_z, own_cols, own_cols),
            ((down, m), high_z, own_cols, own_cols),
            ((g, right), own_z, last_cols, low_cols),
            ((g, left), own_z, first_cols, high_cols),
            ((up, right), low_z, last_cols, low_cols),
            ((up, left), low_z, first_cols, high_cols),
            ((down, right), high_z, last_cols, low_cols),
            ((down, left), high_z, first_cols, high_cols),
        )
    ):
        copy = pltpu.make_async_remote_copy(
            src_ref=field_a.at[:, own_z, here_x, :],
            dst_ref=field_a.at[:, there_z, there_x, :],
            send_sem=hs_sem.at[i],
            recv_sem=hr_sem.at[i],
            device_id=who,
            device_id_type=MESH,
        )
        copy.start()
        margin.append(copy)

    arrived(recv2, 1)
    turned = recv2[:, 0, :].T
    columns = jnp.concatenate([turned[0:16], turned[16:32]], axis=1)
    spectrum = dot(columns, fwd_z[...])
    own_x[...] = spectrum
    gathers = []
    for j in range(1, M):
        copy = pltpu.make_async_remote_copy(
            src_ref=own_x,
            dst_ref=all_x.at[j],
            send_sem=xs_sem.at[j],
            recv_sem=xr_sem.at[j],
            device_id=(g, lax.rem(m + M - j, M)),
            device_id_type=MESH,
        )
        copy.start()
        gathers.append(copy)
    all_x[0] = spectrum
    zero_mode = (iota((128, 256), 0) == 0) & (iota((128, 256), 1) == 0) & (g == 0)
    factor = jnp.where(zero_mode, 0.0, (GRAV / 8.0) / (lam_xz[...] + lam_y[...]))
    for copy in gathers:
        copy.wait_recv()
    filtered = dot(fwd_x[...], all_x[...].reshape(128, 256)) * factor
    wanted = dot(inv_x[...], filtered)
    even, odd = wanted[:, :128], wanted[:, 128:]
    moved = jnp.concatenate(
        [rot_c[...] * even + rot_s[...] * odd, rot_d[...] * odd - rot_s[...] * even], axis=1
    )
    send3[:, 0, :] = dot_t(inv_z[...], moved)
    scatter(send3, recv3, 2)
    arrived(recv3, 2)

    pot_wide = dot(recv3[:, 0, :].T, inv_y[...])
    pot_c[0] = pot_wide[4:20, NY:]
    pot_c[1] = pot_wide[28:44, NY:]
    pot_copy = pltpu.make_async_copy(pot_c, pot_out, out_sem.at[0])
    pot_copy.start()
    for edge in (0, 5):
        pot_v[edge] = jnp.full((2, EXT_X, 128), 3.0, F32)
    for offset, start, rows in PLANE_ROWS:
        block = pot_wide[start : start + rows, :NY] + 3.0
        skip = (24 - rows) // 2 * 2
        for odd_row in range(2):
            for side in range(2):
                half = block[:, side * 128 : (side + 1) * 128]
                pot_v[offset + 2, side, pl.ds(skip + odd_row, rows, stride=2), :] = half

    for copy in margin:
        copy.wait_recv()

    def stage(source, target, length, z, rows):
        top = 0 if rows is None else PAD
        count = EXT_X if rows is None else COLS
        keep = pl.ds(top, count)
        three_plus = jnp.concatenate(
            [pot_v[z // 2, 0, keep, :], pot_v[z // 2, 1, keep, :]], axis=1
        )
        sums, centres = [], []
        for part in range(2):
            whole = source[part, z]
            beside = pltpu.roll(whole, 1, 0) + pltpu.roll(whole, EXT_X - 1, 0)
            centre = source[part, z, keep, :]
            total = (
                (source[part, z - 1, keep, :] + source[part, z + 1, keep, :])
                + beside[top : top + count]
                + (pltpu.roll(centre, 1, 1) + pltpu.roll(centre, NY - 1, 1))
            )
            sums.append(0.5 * total)
            centres.append(centre)
        real = three_plus * centres[1] - sums[1]
        imag = sums[0] - three_plus * centres[0]
        new_real = field_a[0, z, keep, :] + length * real
        new_imag = field_a[1, z, keep, :] + length * imag
        if rows is None:
            target[0, z] = new_real
            target[1, z] = new_imag
        else:
            target[0, z - 4] = new_real
            target[1, z - 4] = new_imag


    def run(source, target, length, margin_z, rows=None):
        def one(z, carry):
            stage(source, target, length, z, rows)
            return carry

        lax.fori_loop(margin_z, EXT_Z - margin_z, one, 0)

    run(field_a, field_b.at[0], STEP_TIME / 4.0, 1)
    run(field_b.at[0], field_b.at[1], STEP_TIME / 3.0, 2)
    run(field_b.at[1], field_b.at[0], STEP_TIME / 2.0, 3)
    run(field_b.at[0], out_v, STEP_TIME, 4, True)
    wave_copy = pltpu.make_async_copy(out_v, wave_out, out_sem.at[1])
    wave_copy.start()

    left_behind(send1, 0)
    left_behind(send2, 1)
    left_behind(send3, 2)
    for copy in gathers + margin:
        copy.wait_send()
    pot_copy.wait()
    wave_copy.wait()


def body(wave, offsets, waves, amps, widths, tile, send_list, send_count):
    given = (
        wave,
        offsets.reshape(3, 1, BEAMS),
        waves.reshape(3, 1, BEAMS),
        amps.reshape(2, 1, BEAMS),
        widths.reshape(1, BEAMS),
        tile.reshape(1, BEAMS),
        send_list.reshape(1, BEAMS),
        send_count.reshape(1, G),
    )
    tabs = tuple(jnp.asarray(t) for t in tables())
    row = (G, 1, 128)
    anywhere = pl.BlockSpec(memory_space=pl.ANY)
    dma = pltpu.SemaphoreType.DMA
    scratch = [pltpu.VMEM(shape, kind) for shape, kind in ARG_SHAPES]
    scratch += [pltpu.VMEM(shape, F32) for shape in TAB_SHAPES]
    scratch += [
        pltpu.VMEM((16, BEAMS), F32),
        pltpu.VMEM((128, 128), F32),
        pltpu.VMEM((128, 128), F32),
    ]
    scratch += [pltpu.VMEM(row, F32)] * 6
    scratch += [pltpu.VMEM((16, 256), F32), pltpu.VMEM((M, 16, 256), F32)]
    scratch += [pltpu.VMEM((256, SLOTS * 256), BF16)] * 4
    scratch += [
        pltpu.VMEM((2, 2 * COLS, 128), F32),
        pltpu.VMEM((6, 2, EXT_X, 128), F32),
        pltpu.VMEM((2, EXT_Z, EXT_X, NY), F32),
        pltpu.VMEM((2, 2, EXT_Z, EXT_X, NY), F32),
        pltpu.VMEM((2, PLANES, COLS, NY), F32),
        pltpu.VMEM((2, 16, 128), F32),
    ]
    scratch += [
        dma((N_ARG,)), dma((N_TAB,)), dma((2,)), dma((3,)), dma((3,)),
        dma((M,)), dma((M,)), dma((8,)), dma((8,)),
    ]
    return pl.pallas_call(
        kernel,
        out_shape=(
            jax.ShapeDtypeStruct((2, PLANES, COLS, NY), F32),
            jax.ShapeDtypeStruct((2, 16, 128), F32),
        ),
        in_specs=[anywhere] * (N_ARG + N_TAB),
        out_specs=(anywhere, anywhere),
        scratch_shapes=scratch,
        compiler_params=pltpu.CompilerParams(
            collective_id=0, has_side_effects=True, vmem_limit_bytes=48 * 1024 * 1024
        ),
    )(*given, *tabs)


def solution(mesh):
    line = P("grp", "mem", None)
    stacked = P(None, "grp", "mem", None)
    return jax.shard_map(
        body,
        mesh=mesh,
        in_specs=(stacked, stacked, stacked, stacked, line, line, line, line),
        out_specs=(stacked, line),
        check_vma=False,
    )
```

time: 219 us -> 82.1 us (0.37)
  the two profiles are of different devices: /device:TPU:14 before, /device:TPU:1 now
where the time goes in v1:
time: 82.1 us; the launch traced here: 81.3 us
  Pallas kernels  64.6 us (79%)
  local copies, waits for them, and re-layouts  16.1 us (20%)
    pallas_call x1, Pallas kernels, body(): pl.pallas_call(kernel, out_shape=(jax.ShapeDtypeStruct((2, PLANES, COLS,...  64.6 us
    unnamed x40, local copies, waits for them, and re-layouts  16.1 us

profile of v1, /device:TPU:1, one launch (start us, length us, event | category | flops | bytes accessed | tf_op | source)
XLA Modules:
  0.0 81.3 jit_solution(1805513291375786433)
XLA Ops:
  0.6 0.0 copy-start.12
  0.6 0.0 copy-start.18
  0.7 0.7 copy-done.12
  1.3 0.0 copy-done.18
  1.3 0.0 copy-start
  1.3 0.9 %copy-done = f32[2,4,32,256]{3,2,1,0:T(8,128)S(1)} copy-done((f32[2,4,32,256]{3,2,1,0:T(8,128)S(1)}, f32[2,4,32,256]{3,2,1,0:T(8,128)}, u32[]{:S(2)}) %copy-start) | copy-done | bytes 262168
  2.3 0.0 copy-start.1
  2.3 0.9 %copy-done.1 = f32[256,256]{1,0:T(8,128)S(1)} copy-done((f32[256,256]{1,0:T(8,128)S(1)}, f32[256,256]{1,0:T(8,128)}, u32[]{:S(2)}) %copy-start.1) | copy-done | bytes 262168
  3.2 0.0 copy-start.2
  3.2 0.9 %copy-done.2 = f32[128,384]{1,0:T(8,128)S(1)} copy-done((f32[128,384]{1,0:T(8,128)S(1)}, f32[128,384]{1,0:T(8,128)}, u32[]{:S(2)}) %copy-start.2) | copy-done | bytes 196632
  4.2 0.0 copy-start.3
  4.2 0.9 %copy-done.3 = f32[128,1,256]{2,1,0:T(1,128)S(1)} copy-done((f32[128,1,256]{2,1,0:T(1,128)S(1)}, f32[128,1,256]{2,1,0:T(1,128)}, u32[]{:S(2)}) %copy-start.3) | copy-done | bytes 131096
  5.1 0.0 copy-start.4
  5.1 0.9 %copy-done.4 = f32[128,256]{1,0:T(8,128)S(1)} copy-done((f32[128,256]{1,0:T(8,128)S(1)}, f32[128,256]{1,0:T(8,128)}, u32[]{:S(2)}) %copy-start.4) | copy-done | bytes 131096
  6.0 0.0 copy-start.5
  6.0 0.9 %copy-done.5 = f32[128,256]{1,0:T(8,128)S(1)} copy-done((f32[128,256]{1,0:T(8,128)S(1)}, f32[128,256]{1,0:T(8,128)}, u32[]{:S(2)}) %copy-start.5) | copy-done | bytes 131096
  6.9 0.0 copy-start.6
  6.9 0.9 %copy-done.6 = f32[128,256]{1,0:T(8,128)S(1)} copy-done((f32[128,256]{1,0:T(8,128)S(1)}, f32[128,256]{1,0:T(8,128)}, u32[]{:S(2)}) %copy-start.6) | copy-done | bytes 131096
  7.8 0.0 copy-start.7
  7.8 0.8 %copy-done.7 = f32[128,128]{1,0:T(8,128)S(1)} copy-done((f32[128,128]{1,0:T(8,128)S(1)}, f32[128,128]{1,0:T(8,128)}, u32[]{:S(2)}) %copy-start.7) | copy-done | bytes 65560
  8.6 0.0 copy-start.8
  8.6 0.8 %copy-done.8 = f32[128,128]{1,0:T(8,128)S(1)} copy-done((f32[128,128]{1,0:T(8,128)S(1)}, f32[128,128]{1,0:T(8,128)}, u32[]{:S(2)}) %copy-start.8) | copy-done | bytes 65560
  9.5 0.0 copy-start.9
  9.5 0.8 %copy-done.9 = f32[128,128]{1,0:T(8,128)S(1)} copy-done((f32[128,128]{1,0:T(8,128)S(1)}, f32[128,128]{1,0:T(8,128)}, u32[]{:S(2)}) %copy-start.9) | copy-done | bytes 65560
  10.3 0.0 copy-start.10
  10.3 0.8 %copy-done.10 = f32[128,128]{1,0:T(8,128)S(1)} copy-done((f32[128,128]{1,0:T(8,128)S(1)}, f32[128,128]{1,0:T(8,128)}, u32[]{:S(2)}) %copy-start.10) | copy-done | bytes 65560
  11.2 0.0 copy-start.11
  11.2 0.8 %copy-done.11 = f32[128,128]{1,0:T(8,128)S(1)} copy-done((f32[128,128]{1,0:T(8,128)S(1)}, f32[128,128]{1,0:T(8,128)}, u32[]{:S(2)}) %copy-start.11) | copy-done | bytes 65560
  12.0 0.0 copy-start.13
  12.0 0.7 copy-done.13
  12.7 0.0 copy-start.14
  12.7 0.7 copy-done.14
  13.4 0.0 copy-start.15
  13.4 0.7 copy-done.15
  14.1 0.0 copy-start.16
  14.1 0.7 copy-done.16
  14.8 0.0 copy-start.17
  14.8 0.7 copy-done.17
  15.5 64.6 %shard_map.194 = (f32[2,4,32,256]{3,2,1,0:T(8,128)S(1)}, f32[2,16,128]{2,1,0:T(8,128)S(1)}) custom-call(f32[2,4,32,256]{3,2,1,0:T(8,128)S(1)} %copy-done, f32[3,1,1024]{2,1,0:T(1,128)S(1)} %bitcast.7, f32[3,1,1024]{2,1,0:T(1,128)S(1)} %bitcast.8, f32[2,1,1024]{2,1,0:T(1,128)S(1)} %bitcast.9, f32[1,1024]{1,0:T(1,128)S(1)} %bitcast.10, ...), custom_call_target="tpu_custom_call" | custom-call | tf_op jit(solution)/shard_map/pallas_call | solution.py:507
  80.0 0.7 copy.23
  80.7 0.6 copy.24
Async XLA Ops:
  0.6 0.7 copy-start.12
  0.6 0.7 copy-start.18
  1.3 1.0 %copy-start = (f32[2,4,32,256]{3,2,1,0:T(8,128)S(1)}, f32[2,4,32,256]{3,2,1,0:T(8,128)}, u32[]{:S(2)}) copy-start(f32[2,4,32,256]{3,2,1,0:T(8,128)} %refs_0_.1) | copy-start | bytes 786436
  2.3 0.9 %copy-start.1 = (f32[256,256]{1,0:T(8,128)S(1)}, f32[256,256]{1,0:T(8,128)}, u32[]{:S(2)}) copy-start(f32[256,256]{1,0:T(8,128)} %constant.23.clone.refs_9_) | copy-start | bytes 786436
  3.2 0.9 %copy-start.2 = (f32[128,384]{1,0:T(8,128)S(1)}, f32[128,384]{1,0:T(8,128)}, u32[]{:S(2)}) copy-start(f32[128,384]{1,0:T(8,128)} %constant.30.clone.refs_16_) | copy-start | bytes 589828
  4.2 0.9 %copy-start.3 = (f32[128,1,256]{2,1,0:T(1,128)S(1)}, f32[128,1,256]{2,1,0:T(1,128)}, u32[]{:S(2)}) copy-start(f32[128,1,256]{2,1,0:T(1,128)} %constant.32.clone.refs_18_) | copy-start | bytes 393220
  5.1 0.9 %copy-start.4 = (f32[128,256]{1,0:T(8,128)S(1)}, f32[128,256]{1,0:T(8,128)}, u32[]{:S(2)}) copy-start(f32[128,256]{1,0:T(8,128)} %constant.31.clone.refs_17_) | copy-start | bytes 393220
  6.0 0.9 %copy-start.5 = (f32[128,256]{1,0:T(8,128)S(1)}, f32[128,256]{1,0:T(8,128)}, u32[]{:S(2)}) copy-start(f32[128,256]{1,0:T(8,128)} %constant.29.clone.refs_15_) | copy-start | bytes 393220
  6.9 0.9 %copy-start.6 = (f32[128,256]{1,0:T(8,128)S(1)}, f32[128,256]{1,0:T(8,128)}, u32[]{:S(2)}) copy-start(f32[128,256]{1,0:T(8,128)} %constant.22.clone.refs_8_) | copy-start | bytes 393220
  7.8 0.8 %copy-start.7 = (f32[128,128]{1,0:T(8,128)S(1)}, f32[128,128]{1,0:T(8,128)}, u32[]{:S(2)}) copy-start(f32[128,128]{1,0:T(8,128)} %constant.28.clone.refs_14_) | copy-start | bytes 196612
  8.6 0.8 %copy-start.8 = (f32[128,128]{1,0:T(8,128)S(1)}, f32[128,128]{1,0:T(8,128)}, u32[]{:S(2)}) copy-start(f32[128,128]{1,0:T(8,128)} %constant.27.clone.refs_13_) | copy-start | bytes 196612
  9.5 0.8 %copy-start.9 = (f32[128,128]{1,0:T(8,128)S(1)}, f32[128,128]{1,0:T(8,128)}, u32[]{:S(2)}) copy-start(f32[128,128]{1,0:T(8,128)} %constant.26.clone.refs_12_) | copy-start | bytes 196612
  10.3 0.8 %copy-start.10 = (f32[128,128]{1,0:T(8,128)S(1)}, f32[128,128]{1,0:T(8,128)}, u32[]{:S(2)}) copy-start(f32[128,128]{1,0:T(8,128)} %constant.25.clone.refs_11_) | copy-start | bytes 196612
  11.2 0.8 %copy-start.11 = (f32[128,128]{1,0:T(8,128)S(1)}, f32[128,128]{1,0:T(8,128)}, u32[]{:S(2)}) copy-start(f32[128,128]{1,0:T(8,128)} %constant.24.clone.refs_10_) | copy-start | bytes 196612
  12.0 0.7 copy-start.13
  12.7 0.7 copy-start.14
  13.4 0.7 copy-start.15
  14.1 0.7 copy-start.16
  14.8 0.7 copy-start.17

commit v2 on v1

--- a/solution.py
+++ b/solution.py
@@ -480,7 +480,7 @@
     )
     tabs = tuple(jnp.asarray(t) for t in tables())
     row = (G, 1, 128)
-    anywhere = pl.BlockSpec(memory_space=pl.ANY)
+    anywhere = pl.BlockSpec(memory_space=pltpu.HBM)
     dma = pltpu.SemaphoreType.DMA
     scratch = [pltpu.VMEM(shape, kind) for shape, kind in ARG_SHAPES]
     scratch += [pltpu.VMEM(shape, F32) for shape in TAB_SHAPES]
@@ -514,7 +514,7 @@
         out_specs=(anywhere, anywhere),
         scratch_shapes=scratch,
         compiler_params=pltpu.CompilerParams(
-            collective_id=0, has_side_effects=True, vmem_limit_bytes=48 * 1024 * 1024
+            collective_id=0, has_side_effects=True, vmem_limit_bytes=67043328
         ),
     )(*given, *tabs)
 

time: 82.1 us -> 68.2 us (0.83)
  local copies, waits for them, and re-layouts: 16.1 us -> 2.29 us
    unnamed x40 -> x4, local copies, waits for them, and re-layouts: 16.1 us -> 2.29 us
where the time goes in v2:
time: 68.2 us; the launch traced here: 68 us
  Pallas kernels  65.1 us (95%)
  local copies, waits for them, and re-layouts  2.29 us (3%)
    pallas_call x1, Pallas kernels, body(): pl.pallas_call(kernel, out_shape=(jax.ShapeDtypeStruct((2, PLANES, COLS,...  65.1 us
    unnamed x4, local copies, waits for them, and re-layouts  2.29 us

profile of v2, /device:TPU:1, one launch (start us, length us, event | category | flops | bytes accessed | tf_op | source)
XLA Modules:
  0.0 68.0 jit_solution(7014765840600271734)
XLA Ops:
  0.6 65.1 %shard_map.194 = (f32[2,4,32,256]{3,2,1,0:T(8,128)}, f32[2,16,128]{2,1,0:T(8,128)}) custom-call(f32[2,4,32,256]{3,2,1,0:T(8,128)} %refs_0_.1, f32[3,1,1024]{2,1,0:T(1,128)} %bitcast.7, f32[3,1,1024]{2,1,0:T(1,128)} %bitcast.8, f32[2,1,1024]{2,1,0:T(1,128)} %bitcast.9, f32[1,1024]{1,0:T(1,128)} %bitcast.10, s32[1,1024]{1,0:T(1,128)} %bitcast.11, ...), custom_call_target="tpu_custom_call" | custom-call | tf_op jit(solution)/shard_map/pallas_call | solution.py:507
  65.7 0.0 copy-start
  65.7 1.7 %copy.23 = f32[2,4,32,256]{3,2,1,0:T(8,128)} copy(f32[2,4,32,256]{3,2,1,0:T(8,128)} %get-tuple-element.4) | data formatting | bytes 524288
  67.4 0.0 copy-done
  67.4 0.6 copy.24
Async XLA Ops:
  65.7 1.7 %copy-start = (f32[2,16,128]{2,1,0:T(8,128)S(1)}, f32[2,16,128]{2,1,0:T(8,128)}, u32[]{:S(2)}) copy-start(f32[2,16,128]{2,1,0:T(8,128)} %get-tuple-element.5) | copy-start | bytes 49156
